TPU v7x, 128 devices: a whole 4x4x4 slice. The times are simulated.
128 devices in a mesh: row: 8 (over z, core), col: 16 (over y, x).
Axes of the slice: x: 4, y: 4, z: 4, core: 2. Of those that a mesh axis runs over, the one named last changes fastest.
Arguments:
- inverse: bfloat16 [18432, 18432], P('row', 'col'), may hold values from -0.046875 to 0.046875
- pair_block: bfloat16 [18432, 2560], P('row', 'col'), may hold values from -6 to 6
- coeffs: bfloat16 [5120, 2560], P('row'), may hold values from -0.125 to 0.125
Outputs:
- gradient_ao: bfloat16 [18432, 5120], P('col', 'row')
All inputs are finite; a program needn't handle non-finite values.
Results may differ from a plain program's by a relative error of at most 0.0049.
Values may be sent and summed in bfloat16 or wider, within the bound.
A program may use at most 128 MiB of HBM per device.

v0:
```python
import jax
import jax.numpy as jnp
from jax import lax
from jax.sharding import PartitionSpec as P


def shards(inverse, pair_block, coeffs):
    cols_here = inverse.shape[1]
    row_count = lax.axis_size("row")
    col_count = lax.axis_size("col")
    blocks_per = col_count // row_count
    col_index = lax.axis_index("col")
    row_index = lax.axis_index("row")
    offset_rows = col_index % blocks_per * cols_here
    holds_diag = col_index // blocks_per == row_index
    columns = lax.all_gather(pair_block, "col", axis=1, tiled=True)
    product = lax.dot_general(
        inverse, columns, (((0,), (0,)), ((), ())), preferred_element_type=jnp.float32
    )
    diagonal = lax.dynamic_slice_in_dim(columns, offset_rows, cols_here, 0).astype(jnp.float32)
    partial_value = product - jnp.where(holds_diag, diagonal, jnp.zeros_like(diagonal))
    portion = lax.psum_scatter(partial_value, "row", scatter_dimension=1, tiled=True)
    gamma_aux = lax.all_gather(portion.astype(jnp.bfloat16), "row", axis=1, tiled=True)
    result = lax.dot_general(
        gamma_aux, coeffs, (((1,), (1,)), ((), ())), preferred_element_type=jnp.float32
    )
    return result.astype(jnp.bfloat16)


def solution(mesh):
    placed = (P("row", "col"), P("row", "col"), P("row", None))
    return jax.shard_map(
        shards, mesh=mesh, in_specs=placed, out_specs=P("col", "row"), check_vma=False
    )
```

profile of v0, /device:TPU:1, one launch (start us, length us, event | category | flops | bytes accessed | tf_op | source)
XLA Modules:
  0.0 247.1 jit_solution(13387108250398124115)
XLA Ops:
  6.5 0.0 copy-start
  6.5 0.0 all-gather.3.cloned.1.call-start
  6.5 0.7 all-gather.3.cloned.1.call-update
  7.3 0.0 reduce-scatter.2.cloned.1.call-start
  7.3 91.7 %all-gather.3.cloned.1.call-done = bf16[2304,2560]{0,1:T(8,128)(2,1)} async-done(((bf16[2304,160]{0,1:T(8,128)(2,1)}), bf16[2304,2560]{0,1:T(8,128)(2,1)}) %all-gather.3.cloned.1.call-update) | async-done | bytes 11796496 | tf_op jit(solution)/shard_map/all_gather | solution.py:16
  99.0 22.4 %convolution_subtract_fusion = f32[1152,2560]{0,1:T(8,128)} fusion(bf16[2304,2560]{0,1:T(8,128)(2,1)} %all-gather.3.cloned.1.call-done, bf16[2304,1152]{1,0:T(8,128)(2,1)} %param.3, s32[]{:T(128)S(6)} %select_n.25, pred[]{:T(512)S(6)} %eq.5), kind=kOutput, calls=%fused_computation | convolution fusion | flops 13598392320 | bytes 34799620 | tf_op jit(solution)/shard_map/dot_general | solution.py:17
  121.4 0.0 reduce-scatter.2.cloned.1.call-update
  121.4 0.0 all-gather.5.cloned.1.call-start
  121.5 68.0 %reduce-scatter.2.cloned.1.call-done = f32[1152,320]{0,1:T(8,128)} async-done(((f32[1152,2560]{0,1:T(8,128)}), f32[1152,320]{0,1:T(8,128)}) %reduce-scatter.2.cloned.1.call-update) | async-done | bytes 1474576 | tf_op jit(solution)/shard_map/reduce_scatter | solution.py:22
  189.5 2.3 convert_element_type.10
  191.8 0.0 all-gather.5.cloned.1.call-update
  191.8 40.2 %all-gather.5.cloned.1.call-done = bf16[1152,2560]{0,1:T(8,128)(2,1)} async-done(((bf16[1152,320]{0,1:T(8,128)(2,1)}), bf16[1152,2560]{0,1:T(8,128)(2,1)}) %all-gather.5.cloned.1.call-update) | async-done | bytes 5898256 | tf_op jit(solution)/shard_map/all_gather | solution.py:23
  232.0 0.0 copy-done
  232.0 8.6 %convolution_convert_fusion = bf16[1152,640]{1,0:T(8,128)(2,1)} fusion(bf16[1152,2560]{0,1:T(8,128)(2,1)} %all-gather.5.cloned.1.call-done, bf16[640,2560]{1,0:T(8,128)(2,1)S(1)} %copy-done), kind=kOutput, calls=%fused_computation.1 | convolution fusion | flops 3775610880 | bytes 10649600 | tf_op jit(solution)/shard_map/dot_general | solution.py:24
Async XLA Ops:
  6.5 225.5 %copy-start = (bf16[640,2560]{1,0:T(8,128)(2,1)S(1)}, bf16[640,2560]{1,0:T(8,128)(2,1)}, u32[]{:S(2)}) copy-start(bf16[640,2560]{1,0:T(8,128)(2,1)} %param.5) | copy-start | bytes 9830404
  6.5 92.5 %all-gather.3.cloned.1.call-start = ((), (), s32[]{:S(2)}) async-start(), calls=%async_computation.1 | async-start | bytes 12533760 | tf_op jit(solution)/shard_map/all_gather | solution.py:16
  7.3 182.2 %reduce-scatter.2.cloned.1.call-start = ((), (), s32[]{:S(2)}) async-start(), calls=%async_computation.2 | async-start | bytes 13271040 | tf_op jit(solution)/shard_map/reduce_scatter | solution.py:22
  121.4 110.6 %all-gather.5.cloned.1.call-start = ((), (), s32[]{:S(2)}) async-start(), calls=%async_computation.3 | async-start | bytes 6635520 | tf_op jit(solution)/shard_map/all_gather | solution.py:23
Sparse Core Ops, SparseCore 0:
  9.5 89.5 all-gather.2
  121.6 67.8 reduce-scatter.1
  191.9 40.0 all-gather.4
where the time goes:
time: 247 us
  waiting for transfers between devices  201 us (81%)
  matrix products  31 us (13%)
  between operations  13.1 us (5%)
    all_gather x1, waiting for transfers between devices, shards(): columns = lax.all_gather(pair_block, 'col', axis=1, tiled=True)  91.7 us
    reduce_scatter x1, waiting for transfers between devices, shards(): lax.psum_scatter(partial_value, 'row', scatter_dimension=1, tiled=True)  68 us
    all_gather x1, waiting for transfers between devices, shards(): lax.all_gather(portion.astype(jnp.bfloat16), 'row', axis=1, tiled=True)  40.2 us
    dot_general x1, matrix products, shards(): lax.dot_general(inverse, columns, (((0,), (0,)), ((), ())), preferred_ele...  22.4 us
    dot_general x1, matrix products, shards(): lax.dot_general(gamma_aux, coeffs, (((1,), (1,)), ((), ())), preferred_el...  8.58 us
  transfers between devices with their start and end apart: 3, of which 3 were waited for; matrix products, arithmetic and copies ran while one was open for 0% of the time, Pallas kernels for 0%

commit v1 on v0

--- a/solution.py
+++ b/solution.py
@@ -13,7 +13,9 @@
     row_index = lax.axis_index("row")
     offset_rows = col_index % blocks_per * cols_here
     holds_diag = col_index // blocks_per == row_index
-    columns = lax.all_gather(pair_block, "col", axis=1, tiled=True)
+    columns = jnp.concatenate(
+        lax.all_to_all(jnp.stack([pair_block] * lax.axis_size("col")), "col", 0, 0), axis=1
+    )
     product = lax.dot_general(
         inverse, columns, (((0,), (0,)), ((), ())), preferred_element_type=jnp.float32
     )

time: 247 us -> 345 us (1.40)
  waiting for transfers between devices: 201 us -> 284 us
  starting transfers between devices: 0.08 us -> 7.71 us
  local copies, waits for them, and re-layouts: 0.01 us -> 6.68 us
    all_to_all x0 -> x1, waiting for transfers between devices: none -> 174 us  [shards(): lax.all_to_all(jnp.stack([pair_block] * lax.axis_size('col')), 'col', 0, 0)]
    all_gather x1 -> x0, waiting for transfers between devices: 91.7 us -> none  [shards(): columns = lax.all_gather(pair_block, 'col', axis=1, tiled=True)]
    all_to_all x0 -> x1, starting transfers between devices: none -> 7.63 us  [shards(): lax.all_to_all(jnp.stack([pair_block] * lax.axis_size('col')), 'col', 0, 0)]
    another operation x0 -> x1, local copies, waits for them, and re-layouts: none -> 6.67 us  [shards(): jnp.stack([pair_block] * lax.axis_size('col'))]
where the time goes in v1:
time: 345 us
  waiting for transfers between devices  284 us (82%)
  matrix products  30.8 us (9%)
  between operations  13.4 us (4%)
  starting transfers between devices  7.71 us (2%)
  local copies, waits for them, and re-layouts  6.68 us (2%)
    all_to_all x1, waiting for transfers between devices, shards(): lax.all_to_all(jnp.stack([pair_block] * lax.axis_size('col')), 'col', 0, 0)  174 us
    reduce_scatter x1, waiting for transfers between devices, shards(): lax.psum_scatter(partial_value, 'row', scatter_dimension=1, tiled=True)  69.6 us
    all_gather x1, waiting for transfers between devices, shards(): lax.all_gather(portion.astype(jnp.bfloat16), 'row', axis=1, tiled=True)  40.2 us
    dot_general x1, matrix products, shards(): lax.dot_general(inverse, columns, (((0,), (0,)), ((), ())), preferred_ele...  22.2 us
    dot_general x1, matrix products, shards(): lax.dot_general(gamma_aux, coeffs, (((1,), (1,)), ((), ())), preferred_el...  8.58 us
    all_to_all x1, starting transfers between devices, shards(): lax.all_to_all(jnp.stack([pair_block] * lax.axis_size('col')), 'col', 0, 0)  7.63 us
  transfers between devices with their start and end apart: 3, of which 3 were waited for; matrix products, arithmetic and copies ran while one was open for 0% of the time, Pallas kernels for 0%

profile of v1, /device:TPU:1, one launch (start us, length us, event | category | flops | bytes accessed | tf_op | source)
XLA Modules:
  0.0 344.7 jit_solution(7795521855280685063)
XLA Ops:
  6.5 0.0 copy-start
  6.5 6.7 %stack.2 = bf16[16,2304,160]{1,2,0:T(8,128)(2,1)} broadcast(bf16[2304,160]{0,1:T(8,128)(2,1)} %param.4), dimensions={1,2} | broadcast | bytes 12533760 | tf_op jit(solution)/shard_map/stack | solution.py:17
  13.2 7.6 %all-to-all-start = ((bf16[16,2304,160]{1,2,0:T(8,128)(2,1)}), bf16[16,2304,160]{1,2,0:T(8,128)(2,1)}, u32[]{:S(2)}, u32[]{:S(2)}) async-start(bf16[16,2304,160]{1,2,0:T(8,128)(2,1)} %stack.2), calls=%async_computation | async-start | bytes 23592960 | tf_op jit(solution)/shard_map/all_to_all | solution.py:17
  20.8 0.0 reduce-scatter.2.cloned.1.call-start
  20.9 173.9 %all-to-all-done = bf16[16,2304,160]{1,2,0:T(8,128)(2,1)} async-done(((bf16[16,2304,160]{1,2,0:T(8,128)(2,1)}), bf16[16,2304,160]{1,2,0:T(8,128)(2,1)}, u32[]{:S(2)}, u32[]{:S(2)}) %all-to-all-start) | async-done | bytes 11796512 | tf_op jit(solution)/shard_map/all_to_all | solution.py:17
  194.9 22.2 %convolution_subtract_fusion = f32[1152,2560]{0,1:T(8,128)} fusion(bf16[2304,2560]{0,1:T(8,128)(2,1)} %bitcast.1, bf16[2304,1152]{1,0:T(8,128)(2,1)} %param.3, s32[]{:T(128)S(6)} %select_n.25, pred[]{:T(512)S(6)} %eq.5), kind=kOutput, calls=%fused_computation | convolution fusion | flops 13598392320 | bytes 34799620 | tf_op jit(solution)/shard_map/dot_general | solution.py:19
  217.1 0.0 reduce-scatter.2.cloned.1.call-update
  217.1 0.0 all-gather.2.cloned.1.call-start
  217.1 69.6 %reduce-scatter.2.cloned.1.call-done = f32[1152,320]{0,1:T(8,128)} async-done(((f32[1152,2560]{0,1:T(8,128)}), f32[1152,320]{0,1:T(8,128)}) %reduce-scatter.2.cloned.1.call-update) | async-done | bytes 1474576 | tf_op jit(solution)/shard_map/reduce_scatter | solution.py:24
  286.7 2.3 convert_element_type.10
  289.0 0.0 all-gather.2.cloned.1.call-update
  289.1 40.2 %all-gather.2.cloned.1.call-done = bf16[1152,2560]{0,1:T(8,128)(2,1)} async-done(((bf16[1152,320]{0,1:T(8,128)(2,1)}), bf16[1152,2560]{0,1:T(8,128)(2,1)}) %all-gather.2.cloned.1.call-update) | async-done | bytes 5898256 | tf_op jit(solution)/shard_map/all_gather | solution.py:25
  329.3 0.0 copy-done
  329.3 8.6 %convolution_convert_fusion = bf16[1152,640]{1,0:T(8,128)(2,1)} fusion(bf16[1152,2560]{0,1:T(8,128)(2,1)} %all-gather.2.cloned.1.call-done, bf16[640,2560]{1,0:T(8,128)(2,1)S(1)} %copy-done), kind=kOutput, calls=%fused_computation.1 | convolution fusion | flops 3775610880 | bytes 10649600 | tf_op jit(solution)/shard_map/dot_general | solution.py:26
Async XLA Ops:
  6.5 322.8 %copy-start = (bf16[640,2560]{1,0:T(8,128)(2,1)S(1)}, bf16[640,2560]{1,0:T(8,128)(2,1)}, u32[]{:S(2)}) copy-start(bf16[640,2560]{1,0:T(8,128)(2,1)} %param.5) | copy-start | bytes 9830404
  13.2 181.7 %all-to-all-start = ((bf16[16,2304,160]{1,2,0:T(8,128)(2,1)}), bf16[16,2304,160]{1,2,0:T(8,128)(2,1)}, u32[]{:S(2)}, u32[]{:S(2)}) async-start(bf16[16,2304,160]{1,2,0:T(8,128)(2,1)} %stack.2), calls=%async_computation | async-start | bytes 23592960 | tf_op jit(solution)/shard_map/all_to_all | solution.py:17
  20.8 265.9 %reduce-scatter.2.cloned.1.call-start = ((), (), s32[]{:S(2)}) async-start(), calls=%async_computation.2 | async-start | bytes 13271040 | tf_op jit(solution)/shard_map/reduce_scatter | solution.py:24
  217.1 112.2 %all-gather.2.cloned.1.call-start = ((), (), s32[]{:S(2)}) async-start(), calls=%async_computation.3 | async-start | bytes 6635520 | tf_op jit(solution)/shard_map/all_gather | solution.py:25
Sparse Core Ops, SparseCore 0:
  217.2 69.4 reduce-scatter.1
  289.2 40.0 all-gather.1
